TPU v7x, 256 devices: a whole 4x4x8 slice. The times are simulated.
256 devices in a mesh: head: 16 (over z, core), tail: 16 (over y, x).
Axes of the slice: x: 4, y: 4, z: 8, core: 2. Of those that a mesh axis runs over, the one named last changes fastest.
Arguments:
- head_emb: bfloat16 [131072, 800], P(('head', 'tail')), may hold values from -48 to 48
- head_state: float32 [131072], P(('head', 'tail')), may hold values from 0.01 to 1
- tail_emb: bfloat16 [64, 128, 800], P('tail'), may hold values from -1.5 to 1.5
- tail_state: float32 [64, 128], P('tail'), may hold values from 0.01 to 1
- relation_emb: bfloat16 [1024, 800], replicated, may hold values from -3.5 to 3.5
- head_rows: int32 [1024, 256], P(('head', 'tail')), may hold values from 0 to 511
- relations: int32 [1024, 256], P(('head', 'tail')), may hold values from 0 to 1023
- tail_offsets: int32 [1024, 256], P(('head', 'tail')), may hold values from 0 to 127
- tail_owner: int32 [1024, 1], P(('head', 'tail')), may hold values from 0 to 15; in each aligned block of 4 rows (0 to 3, 4 to 7, ...) at most 2 rows name the same one
- tail_local: int32 [1024], P(('head', 'tail')), may hold values from 0 to 3
- block_count: int32 [256], P(('head', 'tail')), may hold values from 1 to 4, as said below
- neg_blocks: int32 [8], replicated, may hold values from 0 to 63, as said below
Outputs:
- head_new: bfloat16 [131072, 800], P(('head', 'tail'))
- head_state_new: float32 [131072], P(('head', 'tail'))
- tail_new: bfloat16 [64, 128, 800], P('tail')
- tail_state_new: float32 [64, 128], P('tail')
Inputs may be any that keep to these rules, and one draw needn't show every extreme that they name: `tail_owner`: no tail index owns the tail blocks of more than 2 edge block slots of one device, and in some devices one owns exactly 2. `block_count`: some device has all 4 slots live. `neg_blocks`: distinct tail blocks; the last tail block is always among them.
All inputs are finite; a program needn't handle non-finite values.
Results may differ from a plain program's by a relative error of at most 0.0012.
The roundings to bfloat16 on the way count: a program that leaves them out, or rounds other values in their place, can miss the bound.
Values may be sent and summed in bfloat16 or wider, within the bound.
A program may use at most 128 MiB of HBM per device.

v0:
```python
import jax
import jax.numpy as jnp
from jax import lax
from jax.sharding import PartitionSpec as P

LEARN_RATE = 0.3


def complex_product(left, right):
    half_width = left.shape[-1] // 2
    left_re, left_im = (left[..., :half_width], left[..., half_width:])
    right_re, right_im = (right[..., :half_width], right[..., half_width:])
    return jnp.concatenate(
        [left_re * right_re - left_im * right_im, left_re * right_im + left_im * right_re], axis=-1
    )


def conj_product(left, right):
    half_width = left.shape[-1] // 2
    left_re, left_im = (left[..., :half_width], left[..., half_width:])
    right_re, right_im = (right[..., :half_width], right[..., half_width:])
    return jnp.concatenate(
        [left_re * right_re + left_im * right_im, left_im * right_re - left_re * right_im], axis=-1
    )


def row_adagrad(embedding, adagrad_state, gradient):
    state_next = adagrad_state + jnp.mean(gradient * gradient, axis=-1)
    updated = (
        embedding.astype(jnp.float32) - LEARN_RATE * gradient / jnp.sqrt(state_next)[..., None]
    )
    return (updated.astype(jnp.bfloat16), state_next)


def per_device(
    head_emb,
    head_state,
    tail_emb,
    tail_state,
    relation_emb,
    head_rows,
    relations,
    tail_offsets,
    tail_owner,
    tail_local,
    block_count,
    neg_blocks,
):
    block_total = tail_local.shape[0]
    edge_count = head_rows.shape[1]
    row_width = head_emb.shape[1]
    span_rows = tail_emb.shape[1]
    owned_blocks = tail_emb.shape[0]
    neg_count = neg_blocks.shape[0]
    peer_count = lax.axis_size("tail")
    head_count = lax.axis_size("head")
    tail_rank = lax.axis_index("tail")
    head_rank = lax.axis_index("head")
    piece = span_rows // head_count
    capacity = max(2, (2 * block_total + peer_count - 1) // peer_count)
    owner_rank = tail_owner[:, 0]
    positions = jnp.arange(block_total, dtype=jnp.int32)
    same_owner = owner_rank[:, None] == owner_rank[None, :]
    earlier = positions[None, :] < positions[:, None]
    slot_index = jnp.sum((same_owner & earlier).astype(jnp.int32), axis=1)
    slot_place = owner_rank * capacity + slot_index
    global_block = owner_rank * owned_blocks + tail_local
    slot_ids = (
        jnp.zeros((peer_count * capacity,), jnp.int32)
        .at[slot_place]
        .set(tail_local)
        .reshape(peer_count, capacity)
    )
    incoming_ids = lax.all_to_all(slot_ids, "tail", split_axis=0, concat_axis=0, tiled=True)
    my_rows = lax.dynamic_slice_in_dim(tail_emb, head_rank * piece, piece, axis=1)
    table = lax.all_gather(
        my_rows.reshape(owned_blocks * piece, row_width), ("head", "tail"), axis=0, tiled=True
    )

    def table_row(block, offset):
        return (
            (offset // piece * peer_count + block // owned_blocks) * owned_blocks
            + block % owned_blocks
        ) * piece + offset % piece

    neg_offset = (
        jnp.arange(head_count, dtype=jnp.int32)[:, None, None] * piece
        + jnp.arange(piece, dtype=jnp.int32)[None, None, :]
    )
    neg_index = table_row(neg_blocks[None, :, None], neg_offset).reshape(-1)
    mine_ids = neg_blocks - tail_rank * owned_blocks
    total_edges = block_total * edge_count
    flat_rows = head_rows.reshape(-1)
    block_of = jnp.arange(total_edges, dtype=jnp.int32) // edge_count
    live_rows = (block_of < block_count[0]).astype(jnp.float32)
    tail_index = block_of * span_rows + tail_offsets.reshape(-1)
    vector_index = table_row(global_block[:, None], tail_offsets).reshape(-1)
    relation_vectors = jnp.take(relation_emb, relations.reshape(-1), axis=0)
    head_vectors = jnp.take(head_emb, flat_rows, axis=0)
    query = complex_product(
        head_vectors.astype(jnp.float32), relation_vectors.astype(jnp.float32)
    ).astype(jnp.bfloat16)
    negatives = jnp.take(table, neg_index, axis=0)
    tail_rows = jnp.take(table, vector_index, axis=0)
    query_float = query.astype(jnp.float32)
    positive = jnp.sum(query_float * tail_rows.astype(jnp.float32), axis=1)
    negative = lax.dot_general(
        query, negatives, (((1,), (1,)), ((), ())), preferred_element_type=jnp.float32
    )
    largest = jnp.maximum(positive, jnp.max(negative, axis=1))
    pos_exp = jnp.exp(positive - largest)
    neg_exp = jnp.exp(negative - largest[:, None])
    denominator = pos_exp + jnp.sum(neg_exp, axis=1)
    pos_grad = (pos_exp / denominator - 1.0) * live_rows
    neg_grad = (neg_exp / denominator[:, None] * live_rows[:, None]).astype(jnp.bfloat16)
    tail_part = pos_grad[:, None] * query_float
    block_grad = (
        jnp.zeros((block_total * span_rows, row_width), jnp.float32)
        .at[tail_index]
        .add(tail_part)
        .astype(jnp.bfloat16)
    )
    outgoing = (
        jnp.zeros((peer_count * capacity, span_rows, row_width), jnp.bfloat16)
        .at[slot_place]
        .set(block_grad.reshape(block_total, span_rows, row_width))
    )
    incoming = lax.all_to_all(
        outgoing.reshape(peer_count, capacity, span_rows, row_width),
        "tail",
        split_axis=0,
        concat_axis=0,
        tiled=True,
    )
    neg_part = lax.dot_general(
        neg_grad, query, (((0,), (0,)), ((), ())), preferred_element_type=jnp.float32
    )
    neg_piece = lax.psum_scatter(neg_part, "head", scatter_dimension=0, tiled=True)
    neg_all = lax.psum(neg_piece, "tail").reshape(neg_count, piece, row_width)
    query_grad = pos_grad[:, None] * tail_rows.astype(jnp.float32) + jnp.dot(
        neg_grad, negatives, preferred_element_type=jnp.float32
    )
    head_grad = (
        jnp.zeros(head_emb.shape, jnp.float32)
        .at[flat_rows]
        .add(conj_product(query_grad, relation_vectors.astype(jnp.float32)))
    )
    head_updated, head_state_updated = row_adagrad(head_emb, head_state, head_grad)
    incoming, head_updated = lax.optimization_barrier((incoming, head_updated))
    arrived = incoming.reshape(peer_count * capacity, head_count, piece, row_width)
    arrived_ids = incoming_ids.reshape(-1)
    tail_grad = jnp.stack(
        [
            jnp.sum(
                jnp.where(
                    (arrived_ids == b)[:, None, None, None], arrived.astype(jnp.float32), 0.0
                ),
                axis=0,
            )
            for b in range(owned_blocks)
        ],
        axis=1,
    )
    tail_piece = lax.psum_scatter(
        tail_grad.reshape(head_count * owned_blocks * piece, row_width),
        "head",
        scatter_dimension=0,
        tiled=True,
    ).reshape(owned_blocks, piece, row_width)
    own_negs = jnp.stack(
        [
            jnp.sum(jnp.where((mine_ids == b)[:, None, None], neg_all, 0.0), axis=0)
            for b in range(owned_blocks)
        ],
        axis=0,
    )
    state_rows = lax.dynamic_slice_in_dim(tail_state, head_rank * piece, piece, axis=1)
    tail_updated, tail_state_updated = row_adagrad(my_rows, state_rows, tail_piece + own_negs)
    tail_updated = lax.all_gather(
        tail_updated.reshape(owned_blocks * piece, row_width), "head", axis=0, tiled=True
    )
    tail_updated = (
        tail_updated.reshape(head_count, owned_blocks, piece, row_width)
        .transpose(1, 0, 2, 3)
        .reshape(owned_blocks, span_rows, row_width)
    )
    tail_state_updated = (
        lax.all_gather(tail_state_updated, "head", axis=0, tiled=False)
        .transpose(1, 0, 2)
        .reshape(owned_blocks, span_rows)
    )
    return (head_updated, head_state_updated, tail_updated, tail_state_updated)


def solution(mesh):
    placed = (
        P(("head", "tail"), None),
        P(("head", "tail")),
        P("tail", None, None),
        P("tail", None),
        P(),
        P(("head", "tail"), None),
        P(("head", "tail"), None),
        P(("head", "tail"), None),
        P(("head", "tail"), None),
        P(("head", "tail")),
        P(("head", "tail")),
        P(),
    )
    return jax.shard_map(
        per_device,
        mesh=mesh,
        in_specs=placed,
        out_specs=(
            P(("head", "tail"), None),
            P(("head", "tail")),
            P("tail", None, None),
            P("tail", None),
        ),
        check_vma=False,
    )
```

profile of v0, /device:TPU:1, one launch (start us, length us, event | category | flops | bytes accessed | tf_op | source)
XLA Modules:
  0.0 508.9 jit_solution(6795767045325392924)
XLA Ops:
  11.0 7.6 %all-to-all-start.1 = ((s32[16,1,2]{2,1,0:T(1,128)}), s32[16,1,2]{2,1,0:T(1,128)S(1)}, u32[]{:S(2)}, u32[]{:S(2)}) async-start(s32[16,1,2]{2,1,0:T(1,128)} %bitcast.10), calls=%async_computation.1 | async-start | bytes 16384 | tf_op jit(solution)/shard_map/all_to_all | solution.py:74
  20.5 4.0 gather_fusion
  27.0 3.0 copy.138
  30.0 5.3 %gather_fusion.1 = bf16[1024,800]{1,0:T(8,128)(2,1)} fusion(bf16[1024,800]{1,0:T(8,128)(2,1)S(1)} %copy.138, s32[1024]{0:T(1024)S(1)} %broadcast_clamp_fusion), kind=kCustom, calls=%fused_computation.3 | custom fusion | bytes 3280896 | tf_op jit(solution)/shard_map/jit(_take)/gather | solution.py:98
  35.3 3.9 copy.139
  43.5 95.8 %all-gather.4.cloned.1.call-done = bf16[8192,800]{1,0:T(8,128)(2,1)} async-done(((bf16[32,800]{1,0:T(8,128)(2,1)}), bf16[8192,800]{1,0:T(8,128)(2,1)}) %all-gather.4.cloned.1.call-update) | async-done | bytes 13107216 | tf_op jit(solution)/shard_map/all_gather | solution.py:76
  139.3 12.8 %gather_fusion.2 = bf16[1024,800]{1,0:T(8,128)(2,1)} fusion(bf16[8192,800]{1,0:T(8,128)(2,1)} %all-gather.4.cloned.1.call-done, s32[1024]{0:T(1024)S(1)} %fusion.40), kind=kCustom, calls=%fused_computation.clone | custom fusion | bytes 3280896 | tf_op jit(solution)/shard_map/jit(_take)/gather | solution.py:104
  152.1 3.8 copy.141
  158.0 12.8 %gather_fusion.3 = bf16[1024,800]{1,0:T(8,128)(2,1)} fusion(bf16[8192,800]{1,0:T(8,128)(2,1)} %all-gather.4.cloned.1.call-done, s32[1024]{0:T(1024)S(1)} %fusion.41), kind=kCustom, calls=%fused_computation.1.clone | custom fusion | bytes 3280896 | tf_op jit(solution)/shard_map/jit(_take)/gather | solution.py:103
  170.8 3.9 fusion.54
  177.5 4.2 fusion.52
  183.9 4.9 copy.142
  188.8 10.7 %scatter_custom_fusion = f32[512,800]{1,0:T(8,128)S(1)} fusion(s32[1024]{0:T(1024)S(1)} %bitcast.128, f32[1024,800]{1,0:T(8,128)} %copy.142, f32[]{:T(128)} %constant.175.clone.1), kind=kCustom, calls=%fused_computation.40 | custom fusion | flops 819200 | bytes 1638912 | tf_op jit(solution)/shard_map/scatter-add | solution.py:120
  202.1 3.5 broadcast_in_dim.115
  208.4 5.2 %all-to-all-start = ((bf16[16,2,128,800]{2,3,1,0:T(8,128)(2,1)}), bf16[16,2,128,800]{2,3,1,0:T(8,128)(2,1)}, u32[]{:S(2)}, u32[]{:S(2)}) async-start(bf16[16,2,128,800]{2,3,1,0:T(8,128)(2,1)} %bitcast.93), calls=%async_computation | async-start | bytes 13107200 | tf_op jit(solution)/shard_map/all_to_all | solution.py:128
  214.3 4.5 fusion.6
  221.9 4.9 copy.145
  226.8 10.7 %scatter_custom_fusion.2 = f32[512,800]{1,0:T(8,128)S(1)} fusion(s32[1024]{0:T(1024)S(1)} %bitcast.123, f32[1024,800]{1,0:T(8,128)} %copy.145, f32[]{:T(128)} %constant.175.clone.1), kind=kCustom, calls=%fused_computation.38 | custom fusion | flops 819200 | bytes 1638912 | tf_op jit(solution)/shard_map/scatter-add | solution.py:146
  239.6 71.6 %all-to-all-done = bf16[16,2,128,800]{2,3,1,0:T(8,128)(2,1)} async-done(((bf16[16,2,128,800]{2,3,1,0:T(8,128)(2,1)}), bf16[16,2,128,800]{2,3,1,0:T(8,128)(2,1)}, u32[]{:S(2)}, u32[]{:S(2)}) %all-to-all-start) | async-done | bytes 6553632 | tf_op jit(solution)/shard_map/all_to_all | solution.py:128
  311.3 7.9 %fusion = (f32[128,800]{0,1:T(8,128)S(1)}, f32[128,800]{0,1:T(8,128)S(1)}, f32[128,800]{0,1:T(8,128)S(1)}, f32[128,800]{0,1:T(8,128)S(1)}) fusion(bf16[16,2,128,800]{2,3,1,0:T(8,128)(2,1)} %all-to-all-done, pred[16,2]{1,0:T(8,128)(4,1)S(1)} %copy.148, pred[16,2]{1,0:T(8,128)(4,1)S(1)} %copy.151, pred[16,2]{1,0:T(8,128)(4,1)S(1)} %copy.154, ...), kind=kLoop, calls=%fused_computation.12 | loop fusion | flops 29081600 | bytes 8192128 | tf_op jit(solution)/shard_map/reduce_sum | solution.py:154
  324.0 77.9 %all-reduce.2.cloned.1.call-done = f32[8,8,800]{2,1,0:T(8,128)} async-done(((f32[8,8,800]{2,1,0:T(8,128)}), f32[8,8,800]{2,1,0:T(8,128)}) %all-reduce.2.cloned.1.call-update) | async-done | bytes 204816 | tf_op jit(solution)/shard_map/psum | solution.py:139
  403.0 58.7 %reduce-scatter.3.cloned.1.call-done = f32[32,800]{1,0:T(8,128)} async-done(((f32[512,800]{1,0:T(8,128)}), f32[32,800]{1,0:T(8,128)}) %reduce-scatter.3.cloned.1.call-update) | async-done | bytes 102416 | tf_op jit(solution)/shard_map/reduce_scatter | solution.py:164
  463.0 17.6 %all-gather.1 = f32[16,4,8]{2,1,0:T(4,128)S(1)} all-gather(f32[1,4,8]{2,1,0:T(4,128)S(1)} %get-tuple-element.49), channel_id=2, replica_groups=mesh['head'=16,'tail'=16] {'head'}, dimensions={0}, use_global_device_ids=true | all-gather | bytes 2176 | tf_op jit(solution)/shard_map/all_gather | solution.py:188
  482.2 18.8 %all_gather.13 = bf16[512,800]{1,0:T(8,128)(2,1)S(1)} all-gather(bf16[32,800]{1,0:T(8,128)(2,1)S(1)} %fusion.18), channel_id=1, replica_groups=mesh['head'=16,'tail'=16] {'head'}, dimensions={0}, use_global_device_ids=true | all-gather | bytes 870400 | tf_op jit(solution)/shard_map/all_gather | solution.py:179
  (123 shorter events, 40.0 us)
Async XLA Ops:
  7.2 2.4 copy-start.17
  7.2 2.6 copy-start.16
  7.2 12.1 %copy-start.11 = (s32[4,256]{1,0:T(4,128)S(1)}, s32[4,256]{1,0:T(4,128)}, u32[]{:S(2)}) copy-start(s32[4,256]{1,0:T(4,128)} %param.21) | copy-start | bytes 12292
  7.2 12.2 %copy-start.12 = (s32[4,256]{1,0:T(4,128)S(1)}, s32[4,256]{1,0:T(4,128)}, u32[]{:S(2)}) copy-start(s32[4,256]{1,0:T(4,128)} %param.20) | copy-start | bytes 12292
  7.2 12.3 %copy-start.13 = (s32[4,256]{1,0:T(4,128)S(1)}, s32[4,256]{1,0:T(4,128)}, u32[]{:S(2)}) copy-start(s32[4,256]{1,0:T(4,128)} %param.19) | copy-start | bytes 12292
  7.2 12.3 %copy-start.18 = (s32[8]{0:T(128)S(1)}, s32[8]{0:T(128)}, u32[]{:S(2)}) copy-start(s32[8]{0:T(128)} %param.25) | copy-start | bytes 100
  7.2 12.6 %copy-start.9 = (bf16[512,800]{0,1:T(8,128)(2,1)S(1)}, bf16[512,800]{0,1:T(8,128)(2,1)}, u32[]{:S(2)}) copy-start(bf16[512,800]{0,1:T(8,128)(2,1)} %param.14) | copy-start | bytes 2457604
  7.3 132.1 %all-gather.4.cloned.1.call-start = ((), (), s32[]{:S(2)}) async-start(), calls=%async_computation.4 | async-start | bytes 14737408 | tf_op jit(solution)/shard_map/all_gather | solution.py:76
  11.0 197.3 %all-to-all-start.1 = ((s32[16,1,2]{2,1,0:T(1,128)}), s32[16,1,2]{2,1,0:T(1,128)S(1)}, u32[]{:S(2)}, u32[]{:S(2)}) async-start(s32[16,1,2]{2,1,0:T(1,128)} %bitcast.10), calls=%async_computation.1 | async-start | bytes 16384 | tf_op jit(solution)/shard_map/all_to_all | solution.py:74
  18.6 292.6 %reduce-scatter.5.cloned.1.call-start = ((), (), s32[]{:S(2)}) async-start(), calls=%async_computation.6 | async-start | bytes 3899392 | tf_op jit(solution)/shard_map/reduce_scatter | solution.py:138
  35.3 4.0 copy-start.5
  39.3 1.4 copy-start.6
  40.9 1.7 copy-start.2
  176.2 1.4 copy-start.8
  208.4 5.9 %copy-start.4 = (bf16[1024,800]{0,1:T(8,128)(2,1)S(1)}, bf16[1024,800]{0,1:T(8,128)(2,1)}, u32[]{:S(2)}) copy-start(bf16[1024,800]{0,1:T(8,128)(2,1)} %copy.141) | copy-start | bytes 4915204
  208.4 102.8 %all-to-all-start = ((bf16[16,2,128,800]{2,3,1,0:T(8,128)(2,1)}), bf16[16,2,128,800]{2,3,1,0:T(8,128)(2,1)}, u32[]{:S(2)}, u32[]{:S(2)}) async-start(bf16[16,2,128,800]{2,3,1,0:T(8,128)(2,1)} %bitcast.93), calls=%async_computation | async-start | bytes 13107200 | tf_op jit(solution)/shard_map/all_to_all | solution.py:128
  213.6 188.4 %all-reduce.2.cloned.1.call-start = ((), (), s32[]{:S(2)}) async-start(), calls=%async_computation.7 | async-start | bytes 458752 | tf_op jit(solution)/shard_map/psum | solution.py:139
  214.3 4.5 copy-start.3
  226.8 10.9 %copy-start.15 = (f32[512]{0:T(512)S(1)}, f32[512]{0:T(512)}, u32[]{:S(2)}) copy-start(f32[512]{0:T(512)} %param.15) | copy-start | bytes 6148
  311.3 150.5 %reduce-scatter.3.cloned.1.call-start = ((), (), s32[]{:S(2)}) async-start(), calls=%async_computation.5 | async-start | bytes 1949696 | tf_op jit(solution)/shard_map/reduce_scatter | solution.py:164
  321.6 1.2 copy-start.7
  321.6 141.3 %copy-start.14 = (f32[4,128]{1,0:T(4,128)S(1)}, f32[4,128]{1,0:T(4,128)}, u32[]{:S(2)}) copy-start(f32[4,128]{1,0:T(4,128)} %param.17) | copy-start | bytes 6148
  321.6 159.6 %copy-start.10 = (bf16[4,8,800]{2,1,0:T(8,128)(2,1)S(1)}, bf16[4,8,800]{2,1,0:T(8,128)(2,1)}, u32[]{:S(2)}) copy-start(bf16[4,8,800]{2,1,0:T(8,128)(2,1)} %copy.164) | copy-start | bytes 153604
  482.2 20.1 %copy-start.1 = (bf16[4,128,800]{1,2,0:T(8,128)(2,1)S(1)}, bf16[4,128,800]{1,2,0:T(8,128)(2,1)}, u32[]{:S(2)}) copy-start(bf16[4,128,800]{1,2,0:T(8,128)(2,1)} %param.16) | copy-start | bytes 2457604
  (1 other events, 1.2 us)
Sparse Core Ops, SparseCore 0:
  12.2 127.0 all-gather.3
  181.8 57.1 reduce-scatter.4
  311.4 90.5 all-reduce.1
  404.3 57.3 reduce-scatter.2
where the time goes:
time: 510 us; the launch traced here: 509 us
  waiting for transfers between devices  304 us (60%)
  local copies, waits for them, and re-layouts  81.4 us (16%)
  other arithmetic  46.3 us (9%)
  blocking collectives  36.4 us (7%)
  between operations  14.9 us (3%)
  starting transfers between devices  13.1 us (3%)
  matrix products  12.6 us (2%)
    all_gather x1, waiting for transfers between devices, per_device(): lax.all_gather(my_rows.reshape(owned_blocks * piece, row_width), ('head',...  95.8 us
    psum x1, waiting for transfers between devices, per_device(): neg_all = lax.psum(neg_piece, 'tail').reshape(neg_count, piece, row_width)  77.9 us
    all_to_all x1, waiting for transfers between devices, per_device(): lax.all_to_all(outgoing.reshape(peer_count, capacity, span_rows, row_widt...  71.6 us
    reduce_scatter x1, waiting for transfers between devices, per_device(): lax.psum_scatter(tail_grad.reshape(head_count * owned_blocks * piece, row...  58.7 us
    all_gather x1, blocking collectives, per_device(): lax.all_gather(tail_updated.reshape(owned_blocks * piece, row_width), 'he...  18.8 us
    all_gather x1, blocking collectives, per_device(): lax.all_gather(tail_state_updated, 'head', axis=0, tiled=False)  17.6 us
    gather x2, local copies, waits for them, and re-layouts, per_device(): tail_rows = jnp.take(table, vector_index, axis=0)  16.6 us
    unnamed x49, local copies, waits for them, and re-layouts  13.4 us
  transfers between devices with their start and end apart: 6, of which 4 were waited for; matrix products, arithmetic and copies ran while one was open for 25% of the time, Pallas kernels for 0%

commit v1 on v0

--- a/solution.py
+++ b/solution.py
@@ -136,7 +136,9 @@
         neg_grad, query, (((0,), (0,)), ((), ())), preferred_element_type=jnp.float32
     )
     neg_piece = lax.psum_scatter(neg_part, "head", scatter_dimension=0, tiled=True)
-    neg_all = lax.psum(neg_piece, "tail").reshape(neg_count, piece, row_width)
+    neg_all = jnp.sum(lax.all_gather(neg_piece, "tail"), axis=0).reshape(
+        neg_count, piece, row_width
+    )
     query_grad = pos_grad[:, None] * tail_rows.astype(jnp.float32) + jnp.dot(
         neg_grad, negatives, preferred_element_type=jnp.float32
     )

time: 510 us -> 452 us (0.89)
  waiting for transfers between devices: 304 us -> 246 us
    psum x1 -> x0, waiting for transfers between devices: 77.9 us -> none  [per_device(): neg_all = lax.psum(neg_piece, 'tail').reshape(neg_count, piece, row_width)]
    reduce_scatter x1, waiting for transfers between devices: 0.01 us -> 17 us  [per_device(): lax.psum_scatter(neg_part, 'head', scatter_dimension=0, tiled=True)]
    all_to_all x1, waiting for transfers between devices: 71.6 us -> 55.2 us  [per_device(): lax.all_to_all(outgoing.reshape(peer_count, capacity, span_rows, row_widt...]
    all_gather x0 -> x1, waiting for transfers between devices: none -> 12.7 us  [per_device(): lax.all_gather(neg_piece, 'tail')]
    all_gather x1, waiting for transfers between devices: 95.8 us -> 105 us  [per_device(): lax.all_gather(my_rows.reshape(owned_blocks * piece, row_width), ('head',...]
  transfers between devices with their start and end apart: 6 -> 6, of which waited for: 4 -> 5; matrix products, arithmetic and copies ran while one was open for 25% -> 20% of each run, Pallas kernels for 0% -> 0%
where the time goes in v1:
time: 452 us; the launch traced here: 451 us
  waiting for transfers between devices  246 us (54%)
  local copies, waits for them, and re-layouts  81.4 us (18%)
  other arithmetic  47.6 us (11%)
  blocking collectives  36.4 us (8%)
  between operations  14.9 us (3%)
  matrix products  12.6 us (3%)
  starting transfers between devices  12.2 us (3%)
    all_gather x1, waiting for transfers between devices, per_device(): lax.all_gather(my_rows.reshape(owned_blocks * piece, row_width), ('head',...  105 us
    reduce_scatter x1, waiting for transfers between devices, per_device(): lax.psum_scatter(tail_grad.reshape(head_count * owned_blocks * piece, row...  56.1 us
    all_to_all x1, waiting for transfers between devices, per_device(): lax.all_to_all(outgoing.reshape(peer_count, capacity, span_rows, row_widt...  55.2 us
    all_gather x1, blocking collectives, per_device(): lax.all_gather(tail_updated.reshape(owned_blocks * piece, row_width), 'he...  18.8 us
    all_gather x1, blocking collectives, per_device(): lax.all_gather(tail_state_updated, 'head', axis=0, tiled=False)  17.6 us
    reduce_scatter x1, waiting for transfers between devices, per_device(): lax.psum_scatter(neg_part, 'head', scatter_dimension=0, tiled=True)  17 us
    gather x2, local copies, waits for them, and re-layouts, per_device(): tail_rows = jnp.take(table, vector_index, axis=0)  16.6 us
    unnamed x49, local copies, waits for them, and re-layouts  13.4 us
  transfers between devices with their start and end apart: 6, of which 5 were waited for; matrix products, arithmetic and copies ran while one was open for 20% of the time, Pallas kernels for 0%

profile of v1, /device:TPU:1, one launch (start us, length us, event | category | flops | bytes accessed | tf_op | source)
XLA Modules:
  0.0 451.0 jit_solution(15271585586016614107)
XLA Ops:
  11.4 4.0 gather_fusion
  21.0 5.3 %gather_fusion.1 = bf16[1024,800]{1,0:T(8,128)(2,1)} fusion(bf16[1024,800]{1,0:T(8,128)(2,1)S(1)} %copy.138, s32[1024]{0:T(1024)S(1)} %broadcast_clamp_fusion), kind=kCustom, calls=%fused_computation.3 | custom fusion | bytes 3280896 | tf_op jit(solution)/shard_map/jit(_take)/gather | solution.py:98
  26.2 3.9 copy.139
  34.4 104.9 %all-gather.6.cloned.1.call-done = bf16[8192,800]{1,0:T(8,128)(2,1)} async-done(((bf16[32,800]{1,0:T(8,128)(2,1)}), bf16[8192,800]{1,0:T(8,128)(2,1)}) %all-gather.6.cloned.1.call-update) | async-done | bytes 13107216 | tf_op jit(solution)/shard_map/all_gather | solution.py:76
  139.3 12.8 %gather_fusion.2 = bf16[1024,800]{1,0:T(8,128)(2,1)} fusion(bf16[8192,800]{1,0:T(8,128)(2,1)} %all-gather.6.cloned.1.call-done, s32[1024]{0:T(1024)S(1)} %fusion.44), kind=kCustom, calls=%fused_computation.clone | custom fusion | bytes 3280896 | tf_op jit(solution)/shard_map/jit(_take)/gather | solution.py:104
  152.2 3.8 copy.141
  158.0 12.8 %gather_fusion.3 = bf16[1024,800]{1,0:T(8,128)(2,1)} fusion(bf16[8192,800]{1,0:T(8,128)(2,1)} %all-gather.6.cloned.1.call-done, s32[1024]{0:T(1024)S(1)} %fusion.45), kind=kCustom, calls=%fused_computation.1.clone | custom fusion | bytes 3280896 | tf_op jit(solution)/shard_map/jit(_take)/gather | solution.py:103
  170.8 3.9 fusion.58
  177.5 4.2 fusion.56
  183.2 5.0 %all-to-all-start.1 = ((s32[16,1,2]{2,1,0:T(1,128)}), s32[16,1,2]{2,1,0:T(1,128)S(1)}, u32[]{:S(2)}, u32[]{:S(2)}) async-start(s32[16,1,2]{2,1,0:T(1,128)} %bitcast.10), calls=%async_computation.1 | async-start | bytes 16384 | tf_op jit(solution)/shard_map/all_to_all | solution.py:74
  190.4 4.9 %copy.142 = f32[1024,800]{1,0:T(8,128)} copy(f32[1024,800]{0,1:T(8,128)} %convert_multiply_fusion.2) | data formatting | bytes 6553600 | tf_op jit(solution)/shard_map/mul | solution.py:116
  195.3 10.7 %scatter_custom_fusion = f32[512,800]{1,0:T(8,128)S(1)} fusion(s32[1024]{0:T(1024)S(1)} %bitcast.141, f32[1024,800]{1,0:T(8,128)} %copy.142, f32[]{:T(128)} %constant.175.clone.1), kind=kCustom, calls=%fused_computation.40 | custom fusion | flops 819200 | bytes 1638912 | tf_op jit(solution)/shard_map/scatter-add | solution.py:120
  208.5 3.5 broadcast_in_dim.115
  214.8 6.9 %all-to-all-start = ((bf16[16,2,128,800]{2,3,1,0:T(8,128)(2,1)}), bf16[16,2,128,800]{2,3,1,0:T(8,128)(2,1)}, u32[]{:S(2)}, u32[]{:S(2)}) async-start(bf16[16,2,128,800]{2,3,1,0:T(8,128)(2,1)} %bitcast.106), calls=%async_computation | async-start | bytes 13107200 | tf_op jit(solution)/shard_map/all_to_all | solution.py:128
  221.8 17.0 %reduce-scatter.5.cloned.1.call-done = f32[64,800]{1,0:T(8,128)} async-done(((f32[1024,800]{1,0:T(8,128)}), f32[64,800]{1,0:T(8,128)}) %reduce-scatter.5.cloned.1.call-update) | async-done | bytes 204816 | tf_op jit(solution)/shard_map/reduce_scatter | solution.py:138
  239.5 4.5 %fusion.6 = f32[1024,800]{0,1:T(8,128)S(1)} fusion(bf16[1024,1024]{0,1:T(8,128)(2,1)} %copy-done.8, f32[1024]{0:T(1024)S(1)} %get-tuple-element.48, bf16[1024,800]{0,1:T(8,128)(2,1)S(1)} %copy-done.4, pred[1024]{0:T(1024)(128)(4,1)S(1)} %get-tuple-element.65, bf16[1024,800]{1,0:T(8,128)(2,1)} %gather_fusion.3, pred[1024]{0:T(1024)(128)(4,1)S(1)} %get-tuple-element.64), kind=kOutput, calls=%fused_computation.23 | convolution fusion | flops 1681817600 | bytes 8656896 | tf_op jit(solution)/shard_map/dot_general | solution.py:142
  247.1 4.9 %copy.145 = f32[1024,800]{1,0:T(8,128)} copy(f32[1024,800]{0,1:T(8,128)} %pad_maximum_fusion) | data formatting | bytes 6553600 | tf_op jit(solution)/shard_map/concatenate | solution.py:22
  252.0 10.7 %scatter_custom_fusion.2 = f32[512,800]{1,0:T(8,128)S(1)} fusion(s32[1024]{0:T(1024)S(1)} %bitcast.136, f32[1024,800]{1,0:T(8,128)} %copy.145, f32[]{:T(128)} %constant.175.clone.1), kind=kCustom, calls=%fused_computation.38 | custom fusion | flops 819200 | bytes 1638912 | tf_op jit(solution)/shard_map/scatter-add | solution.py:148
  264.8 55.2 %all-to-all-done = bf16[16,2,128,800]{2,3,1,0:T(8,128)(2,1)} async-done(((bf16[16,2,128,800]{2,3,1,0:T(8,128)(2,1)}), bf16[16,2,128,800]{2,3,1,0:T(8,128)(2,1)}, u32[]{:S(2)}, u32[]{:S(2)}) %all-to-all-start) | async-done | bytes 6553632 | tf_op jit(solution)/shard_map/all_to_all | solution.py:128
  320.0 7.9 %fusion = (f32[128,800]{0,1:T(8,128)S(1)}, f32[128,800]{0,1:T(8,128)S(1)}, f32[128,800]{0,1:T(8,128)S(1)}, f32[128,800]{0,1:T(8,128)S(1)}) fusion(bf16[16,2,128,800]{2,3,1,0:T(8,128)(2,1)} %all-to-all-done, pred[16,2]{1,0:T(8,128)(4,1)S(1)} %copy.148, pred[16,2]{1,0:T(8,128)(4,1)S(1)} %copy.151, pred[16,2]{1,0:T(8,128)(4,1)S(1)} %copy.154, ...), kind=kLoop, calls=%fused_computation.12 | loop fusion | flops 29081600 | bytes 8192128 | tf_op jit(solution)/shard_map/reduce_sum | solution.py:156
  332.7 12.7 %all-gather.8.cloned.1.call-done = f32[1024,800]{1,0:T(8,128)} async-done(((f32[64,800]{1,0:T(8,128)}), f32[1024,800]{1,0:T(8,128)}) %all-gather.8.cloned.1.call-update) | async-done | bytes 3276816 | tf_op jit(solution)/shard_map/all_gather | solution.py:139
  347.8 56.1 %reduce-scatter.3.cloned.1.call-done = f32[32,800]{1,0:T(8,128)} async-done(((f32[512,800]{1,0:T(8,128)}), f32[32,800]{1,0:T(8,128)}) %reduce-scatter.3.cloned.1.call-update) | async-done | bytes 102416 | tf_op jit(solution)/shard_map/reduce_scatter | solution.py:166
  405.0 17.6 %all-gather.2 = f32[16,4,8]{2,1,0:T(4,128)S(1)} all-gather(f32[1,4,8]{2,1,0:T(4,128)S(1)} %get-tuple-element.49), channel_id=3, replica_groups=mesh['head'=16,'tail'=16] {'head'}, dimensions={0}, use_global_device_ids=true | all-gather | bytes 2176 | tf_op jit(solution)/shard_map/all_gather | solution.py:190
  424.3 18.8 %all_gather.21 = bf16[512,800]{1,0:T(8,128)(2,1)S(1)} all-gather(bf16[32,800]{1,0:T(8,128)(2,1)S(1)} %fusion.22), channel_id=1, replica_groups=mesh['head'=16,'tail'=16] {'head'}, dimensions={0}, use_global_device_ids=true | all-gather | bytes 870400 | tf_op jit(solution)/shard_map/all_gather | solution.py:181
  (124 shorter events, 44.3 us)
Async XLA Ops:
  7.2 3.1 copy-start.16
  7.2 3.1 copy-start.17
  7.2 3.1 copy-start.13
  7.2 3.2 copy-start.11
  7.2 3.2 copy-start.12
  7.2 3.2 copy-start.18
  7.2 3.5 copy-start.9
  7.3 132.1 %all-gather.6.cloned.1.call-start = ((), (), s32[]{:S(2)}) async-start(), calls=%async_computation.4 | async-start | bytes 14737408 | tf_op jit(solution)/shard_map/all_gather | solution.py:76
  9.5 229.2 %reduce-scatter.5.cloned.1.call-start = ((), (), s32[]{:S(2)}) async-start(), calls=%async_computation.6 | async-start | bytes 3899392 | tf_op jit(solution)/shard_map/reduce_scatter | solution.py:138
  26.2 4.0 copy-start.5
  30.2 1.4 copy-start.6
  31.9 1.7 copy-start.2
  176.2 1.4 copy-start.8
  183.2 31.6 %all-to-all-start.1 = ((s32[16,1,2]{2,1,0:T(1,128)}), s32[16,1,2]{2,1,0:T(1,128)S(1)}, u32[]{:S(2)}, u32[]{:S(2)}) async-start(s32[16,1,2]{2,1,0:T(1,128)} %bitcast.10), calls=%async_computation.1 | async-start | bytes 16384 | tf_op jit(solution)/shard_map/all_to_all | solution.py:74
  214.8 24.7 %copy-start.4 = (bf16[1024,800]{0,1:T(8,128)(2,1)S(1)}, bf16[1024,800]{0,1:T(8,128)(2,1)}, u32[]{:S(2)}) copy-start(bf16[1024,800]{0,1:T(8,128)(2,1)} %copy.141) | copy-start | bytes 4915204
  214.8 105.2 %all-to-all-start = ((bf16[16,2,128,800]{2,3,1,0:T(8,128)(2,1)}), bf16[16,2,128,800]{2,3,1,0:T(8,128)(2,1)}, u32[]{:S(2)}, u32[]{:S(2)}) async-start(bf16[16,2,128,800]{2,3,1,0:T(8,128)(2,1)} %bitcast.106), calls=%async_computation | async-start | bytes 13107200 | tf_op jit(solution)/shard_map/all_to_all | solution.py:128
  221.7 123.7 %all-gather.8.cloned.1.call-start = ((), (), s32[]{:S(2)}) async-start(), calls=%async_computation.7 | async-start | bytes 3899392 | tf_op jit(solution)/shard_map/all_gather | solution.py:139
  238.7 165.1 %reduce-scatter.3.cloned.1.call-start = ((), (), s32[]{:S(2)}) async-start(), calls=%async_computation.5 | async-start | bytes 1949696 | tf_op jit(solution)/shard_map/reduce_scatter | solution.py:166
  239.5 4.5 %copy-start.3 = (f32[1024,800]{0,1:T(8,128)S(1)}, f32[1024,800]{0,1:T(8,128)}, u32[]{:S(2)}) copy-start(f32[1024,800]{0,1:T(8,128)} %copy-done.2) | copy-start | bytes 9830404
  252.0 10.9 %copy-start.15 = (f32[512]{0:T(512)S(1)}, f32[512]{0:T(512)}, u32[]{:S(2)}) copy-start(f32[512]{0:T(512)} %param.15) | copy-start | bytes 6148
  330.3 1.2 copy-start.7
  345.4 59.6 %copy-start.14 = (f32[4,128]{1,0:T(4,128)S(1)}, f32[4,128]{1,0:T(4,128)}, u32[]{:S(2)}) copy-start(f32[4,128]{1,0:T(4,128)} %param.17) | copy-start | bytes 6148
  345.4 78.0 %copy-start.10 = (bf16[4,8,800]{2,1,0:T(8,128)(2,1)S(1)}, bf16[4,8,800]{2,1,0:T(8,128)(2,1)}, u32[]{:S(2)}) copy-start(bf16[4,8,800]{2,1,0:T(8,128)(2,1)} %copy.164) | copy-start | bytes 153604
  424.3 20.1 %copy-start.1 = (bf16[4,128,800]{1,2,0:T(8,128)(2,1)S(1)}, bf16[4,128,800]{1,2,0:T(8,128)(2,1)}, u32[]{:S(2)}) copy-start(bf16[4,128,800]{1,2,0:T(8,128)(2,1)} %param.16) | copy-start | bytes 2457604
  (1 other events, 1.2 us)
Sparse Core Ops, SparseCore 0:
  12.2 127.0 all-gather.5
  181.8 56.8 reduce-scatter.4
  241.1 104.1 all-gather.7
  347.8 56.0 reduce-scatter.2
